TPU v7x, 32 devices: a whole 2x2x4 slice. The times are simulated.
32 devices in a mesh: expert: 4 (over x, core), dp: 8 (over z, y).
Axes of the slice: x: 2, y: 2, z: 4, core: 2. Of those that a mesh axis runs over, the one named last changes fastest.
Arguments:
- layer_input: bfloat16 [8192, 768], P(('expert', 'dp')), may hold values from -6 to 6
- routes: int32 [8192, 2], P(('expert', 'dp')), may hold values from 0 to 15, all different within a row
- priority: int32 [32, 512], P(('expert', 'dp')), may hold values from 0 to 511, each once within a row
- cont_ids: int32 [32, 128], P(('expert', 'dp')), may hold values from 0 to 3, never falling along the last dimension, each value on 1 to 64 neighbouring positions
- cotangent: bfloat16 [8192, 768], P(('expert', 'dp')), may hold values from -6 to 6
- norm1_gain: bfloat16 [768], P('dp'), may hold values from 0.099609375 to 1.8984375
- qkv_weight: bfloat16 [768, 2304], P('dp'), may hold values from -0.21875 to 0.21875
- out_weight: bfloat16 [768, 768], P('dp'), may hold values from -0.875 to 0.875
- norm2_gain: bfloat16 [768], P('dp'), may hold values from 0.099609375 to 1.8984375
- router_weight: bfloat16 [768, 16], P('dp'), may hold values from -0.109375 to 0.109375
- shared_in: bfloat16 [768, 4096], P('dp'), may hold values from -0.21875 to 0.21875
- shared_out: bfloat16 [2048, 768], P('dp'), may hold values from -0.125 to 0.125
- expert_in: bfloat16 [16, 768, 4096], P('expert', 'dp'), may hold values from -0.21875 to 0.21875
- expert_out: bfloat16 [16, 2048, 768], P('expert', 'dp'), may hold values from -0.1875 to 0.1875
Outputs:
- layer_output: bfloat16 [8192, 768], P(('expert', 'dp'))
- input_grad: float32 [8192, 768], P(('expert', 'dp'))
- norm1_grad: float32 [768], P('dp')
- qkv_grad: float32 [768, 2304], P('dp')
- out_weight_grad: float32 [768, 768], P('dp')
- norm2_grad: float32 [768], P('dp')
- router_grad: float32 [768, 16], P('dp')
- shared_in_grad: float32 [768, 4096], P('dp')
- shared_out_grad: float32 [2048, 768], P('dp')
- expert_in_grad: float32 [16, 768, 4096], P('expert', 'dp')
- expert_out_grad: float32 [16, 2048, 768], P('expert', 'dp')
Inputs may be any that keep to these rules, and one draw needn't show every extreme that they name: `routes`: each token names 2 different experts. `priority`: each row is a permutation of the 512 pairs of its group. `cont_ids`: each row never falls; each of the 4 continuations has 1 to 64 tokens, one exactly 64.
All inputs are finite; a program needn't handle non-finite values.
Results may differ from a plain program's by a relative error of at most 0.02.
Values may be sent and summed in bfloat16 or wider, within the bound.
No kernel may reach another device: no remote copies, remote signals or barrier semaphores. Data moves between devices by JAX's collectives and lax.ppermute only.
A program may use at most 192 MiB of HBM per device.

v0:
```python
from functools import partial

import jax
import jax.numpy as jnp
from jax import lax
from jax.sharding import PartitionSpec as P

D = 768
HEADS = 12
HEAD = 64
EXPERTS = 16
FF = 2048
TOP = 2
FS = 2048
CONTS = 4
TOK_DEV = 256
PROMPT = 128
CAP = 40


epsilon = 1e-06
rope_base = 10000.0
highest = lax.Precision.HIGHEST
bfloat = jnp.bfloat16
single = jnp.float32


def layout(cont_row):
    labels = jnp.arange(CONTS, dtype=jnp.int32)
    member = cont_row[:, None] == labels[None, :]
    lengths = jnp.sum(member.astype(jnp.int32), axis=0)
    starts = jnp.cumsum(lengths) - lengths
    begins = jnp.sum(jnp.where(member, starts[None, :], 0), axis=1)
    offsets = jnp.arange(cont_row.shape[0], dtype=jnp.int32) - begins
    position = jnp.concatenate([jnp.arange(PROMPT, dtype=jnp.int32), PROMPT + offsets])
    segment = jnp.concatenate([jnp.full((PROMPT,), -1, jnp.int32), cont_row])
    rows_at = jnp.arange(TOK_DEV, dtype=jnp.int32)
    visible = (rows_at[None, :] <= rows_at[:, None]) & (segment[None, :] == segment[:, None]) | (
        rows_at[None, :] < PROMPT
    ) & (rows_at[:, None] >= PROMPT)
    half_dim = HEAD // 2
    frequency = rope_base ** (-(jnp.arange(half_dim, dtype=single) * 2.0) / HEAD)
    angles = position.astype(single)[:, None] * frequency[None, :]
    cosine = jnp.concatenate([jnp.cos(angles), jnp.cos(angles)], axis=1)
    sine_table = jnp.concatenate([jnp.sin(angles), jnp.sin(angles)], axis=1)
    return (visible, cosine, sine_table)


def rotate(values, cosine, sine_table):
    half_dim = HEAD // 2
    turned = jnp.concatenate([-values[..., half_dim:], values[..., :half_dim]], axis=-1)
    return values * cosine[:, None, :] + turned * sine_table[:, None, :]


def unrotate(gradient, cosine, sine_table):
    half_dim = HEAD // 2
    turned = jnp.concatenate([gradient[..., half_dim:], -gradient[..., :half_dim]], axis=-1)
    return gradient * cosine[:, None, :] + turned * sine_table[:, None, :]


def swish(gate_part):
    return gate_part * jax.nn.sigmoid(gate_part)


def swish_slope(gate_part):
    sigmoid_value = jax.nn.sigmoid(gate_part)
    return sigmoid_value * (1.0 + gate_part * (1.0 - sigmoid_value))


def slot_plan(route_rows, prio_row):
    pair_expert = route_rows.reshape(-1)
    onehot = (pair_expert[:, None] == jnp.arange(EXPERTS, dtype=jnp.int32)[None, :]).astype(
        jnp.int32
    )
    ordered = jnp.zeros_like(onehot).at[prio_row].set(onehot)
    before = jnp.cumsum(ordered, axis=0) - ordered
    slot_index = jnp.sum(before[prio_row] * onehot, axis=1)
    return (pair_expert, slot_index)


def pair_forward(visible, pieces):
    query_pair, key_pair, value_pair = pieces
    scores = jnp.einsum("qhd,khd->hqk", query_pair, key_pair, preferred_element_type=single) * 0.125
    scores = jnp.where(visible[None], scores, -1e30)
    top_score = jnp.max(scores, axis=-1, keepdims=True)
    weights = jnp.exp(scores - top_score)
    totals = jnp.sum(weights, axis=-1, keepdims=True)
    attention = (weights / totals).astype(bfloat)
    context = jnp.einsum("hqk,khd->qhd", attention, value_pair, preferred_element_type=single)
    return (context.astype(bfloat), (top_score + jnp.log(totals))[..., 0])


def pair_backward(visible, pieces):
    query_pair, key_pair, value_pair, log_total, grad_context = pieces
    scores = jnp.einsum("qhd,khd->hqk", query_pair, key_pair, preferred_element_type=single) * 0.125
    scores = jnp.where(visible[None], scores, -1e30)
    attention = jnp.exp(scores - log_total[..., None])
    attention_low = attention.astype(bfloat)
    grad_value = jnp.einsum(
        "hqk,qhd->khd", attention_low, grad_context, preferred_element_type=single
    )
    grad_attention = jnp.einsum(
        "qhd,khd->hqk", grad_context, value_pair, preferred_element_type=single
    )
    grad_scores = (
        attention * (grad_attention - jnp.sum(attention * grad_attention, axis=-1, keepdims=True))
    ).astype(bfloat)
    grad_query = (
        jnp.einsum("hqk,khd->qhd", grad_scores, key_pair, preferred_element_type=single) * 0.125
    )
    grad_key = (
        jnp.einsum("hqk,qhd->khd", grad_scores, query_pair, preferred_element_type=single) * 0.125
    )
    return (grad_query, grad_key, grad_value)


def local(
    layer_input,
    routes,
    priority,
    cont_ids,
    cotangent,
    norm1_gain,
    qkv_weight,
    out_weight,
    norm2_gain,
    router_weight,
    shared_in,
    shared_out,
    expert_in,
    expert_out,
):
    gathered = (
        lax.all_gather(norm1_gain, "dp", axis=0, tiled=True),
        lax.all_gather(qkv_weight, "dp", axis=0, tiled=True),
        lax.all_gather(out_weight, "dp", axis=0, tiled=True),
        lax.all_gather(norm2_gain, "dp", axis=0, tiled=True),
        lax.all_gather(router_weight, "dp", axis=0, tiled=True),
        lax.all_gather(shared_in, "dp", axis=0, tiled=True),
        lax.all_gather(shared_out, "dp", axis=0, tiled=True),
        lax.all_gather(expert_in, "dp", axis=1, tiled=True),
        lax.all_gather(expert_out, "dp", axis=1, tiled=True),
    )
    (
        gain_one,
        qkv_full,
        outw_full,
        gain_two,
        router_full,
        shared_wide,
        shared_down,
        expert_wide,
        expert_down,
    ) = gathered
    row_count = layer_input.shape[0]
    expert_groups = lax.axis_size("expert")
    local_experts = EXPERTS // expert_groups
    visible, cosine, sine_table = layout(cont_ids[0])

    def by_pairs(stacked):
        return jnp.moveaxis(stacked.reshape(row_count, HEADS // 2, 2, HEAD), 1, 0)

    def from_pairs(stacked):
        return jnp.moveaxis(stacked, 0, 1).reshape(row_count, D)

    inputs = layer_input.astype(single)
    scale_one = lax.rsqrt(jnp.mean(inputs * inputs, axis=-1, keepdims=True) + epsilon)
    normal_one = inputs * scale_one
    hidden_one = (normal_one * gain_one.astype(single)).astype(bfloat)
    projected = jnp.dot(hidden_one, qkv_full, preferred_element_type=single)
    queries = rotate(projected[:, :D].reshape(row_count, HEADS, HEAD), cosine, sine_table).astype(
        bfloat
    )
    key_heads = rotate(
        projected[:, D : 2 * D].reshape(row_count, HEADS, HEAD), cosine, sine_table
    ).astype(bfloat)
    values = projected[:, 2 * D :].astype(bfloat)
    context_pairs, log_totals = lax.map(
        partial(pair_forward, visible), (by_pairs(queries), by_pairs(key_heads), by_pairs(values))
    )
    context = from_pairs(context_pairs)
    residual = inputs + jnp.dot(context, outw_full, preferred_element_type=single)
    scale_two = lax.rsqrt(jnp.mean(residual * residual, axis=-1, keepdims=True) + epsilon)
    normal_two = residual * scale_two
    hidden_two = (normal_two * gain_two.astype(single)).astype(bfloat)
    hidden_wide = hidden_two.astype(single)
    router_wide = router_full.astype(single)
    gate_probs = jax.nn.softmax(jnp.dot(hidden_wide, router_wide, precision=highest), axis=-1)
    shared_pre = jnp.dot(hidden_two, shared_wide, preferred_element_type=single)
    shared_hidden = (swish(shared_pre[:, :FS]) * shared_pre[:, FS:]).astype(bfloat)
    shared_part = jnp.dot(shared_hidden, shared_down, preferred_element_type=single)
    pair_expert, slot_index = slot_plan(routes, priority[0])
    pair_count = row_count * TOP
    kept_mask = slot_index < CAP
    flat_slot = jnp.where(kept_mask, pair_expert * CAP + slot_index, EXPERTS * CAP)
    slot_pair = (
        jnp.full((EXPERTS * CAP + 1,), pair_count, jnp.int32)
        .at[flat_slot]
        .set(jnp.arange(pair_count, dtype=jnp.int32))[: EXPERTS * CAP]
    )
    slot_token = slot_pair // TOP
    send_rows = jnp.take(hidden_two, slot_token, axis=0, mode="fill", fill_value=0).reshape(
        expert_groups, local_experts, CAP, D
    )
    arrived = lax.all_to_all(send_rows, "expert", split_axis=0, concat_axis=0, tiled=True)
    expert_pre = jnp.einsum("secd,edf->secf", arrived, expert_wide, preferred_element_type=single)
    expert_hidden = (swish(expert_pre[..., :FF]) * expert_pre[..., FF:]).astype(bfloat)
    expert_result = jnp.einsum(
        "secf,efd->secd", expert_hidden, expert_down, preferred_element_type=single
    ).astype(bfloat)
    returned = lax.all_to_all(
        expert_result, "expert", split_axis=0, concat_axis=0, tiled=True
    ).reshape(EXPERTS * CAP, D)
    pair_result = jnp.take(returned, flat_slot, axis=0, mode="fill", fill_value=0).astype(single)
    pair_gate = jnp.take_along_axis(gate_probs, routes, axis=1).reshape(-1)
    routed = jnp.sum((pair_gate[:, None] * pair_result).reshape(row_count, TOP, D), axis=1)
    output = (residual + shared_part + routed).astype(bfloat)
    gathered = (
        lax.all_gather(norm1_gain, "dp", axis=0, tiled=True),
        lax.all_gather(qkv_weight, "dp", axis=0, tiled=True),
        lax.all_gather(out_weight, "dp", axis=0, tiled=True),
        lax.all_gather(norm2_gain, "dp", axis=0, tiled=True),
        lax.all_gather(router_weight, "dp", axis=0, tiled=True),
        lax.all_gather(shared_in, "dp", axis=0, tiled=True),
        lax.all_gather(shared_out, "dp", axis=0, tiled=True),
        lax.all_gather(expert_in, "dp", axis=1, tiled=True),
        lax.all_gather(expert_out, "dp", axis=1, tiled=True),
    )
    (
        gain_one,
        qkv_full,
        outw_full,
        gain_two,
        router_full,
        shared_wide,
        shared_down,
        expert_wide,
        expert_down,
    ) = gathered
    router_wide = router_full.astype(single)
    grad_output = cotangent.astype(single)
    token_grad = jnp.repeat(grad_output, TOP, axis=0)
    grad_gate_pair = jnp.sum(token_grad * pair_result, axis=-1).reshape(row_count, TOP)
    expert_ids = jnp.arange(EXPERTS, dtype=jnp.int32)
    grad_gates = jnp.sum(
        jnp.where(routes[:, :, None] == expert_ids[None, None, :], grad_gate_pair[:, :, None], 0.0),
        axis=1,
    )
    grad_logits = gate_probs * (
        grad_gates - jnp.sum(gate_probs * grad_gates, axis=-1, keepdims=True)
    )
    router_grad = jnp.einsum("td,te->de", hidden_wide, grad_logits, precision=highest)
    pair_grad = (pair_gate[:, None] * token_grad).astype(bfloat)
    slot_grad = jnp.take(pair_grad, slot_pair, axis=0, mode="fill", fill_value=0).reshape(
        expert_groups, local_experts, CAP, D
    )
    grad_arrived = lax.all_to_all(slot_grad, "expert", split_axis=0, concat_axis=0, tiled=True)
    grad_expert_hidden = jnp.einsum(
        "secd,efd->secf", grad_arrived, expert_down, preferred_element_type=single
    )
    expert_out_grad = jnp.einsum(
        "secf,secd->efd", expert_hidden, grad_arrived, preferred_element_type=single
    )
    expert_gate = expert_pre[..., :FF]
    expert_up = expert_pre[..., FF:]
    grad_expert_pre = jnp.concatenate(
        [
            grad_expert_hidden * expert_up * swish_slope(expert_gate),
            grad_expert_hidden * swish(expert_gate),
        ],
        axis=-1,
    ).astype(bfloat)
    expert_in_grad = jnp.einsum(
        "secd,secf->edf", arrived, grad_expert_pre, preferred_element_type=single
    )
    grad_rows = jnp.einsum(
        "secf,edf->secd", grad_expert_pre, expert_wide, preferred_element_type=single
    ).astype(bfloat)
    grad_back = (
        lax.all_to_all(grad_rows, "expert", split_axis=0, concat_axis=0, tiled=True)
        .reshape(EXPERTS * CAP, D)
        .astype(single)
    )
    grad_hidden_two = (
        jnp.zeros((row_count + 1, D), single).at[slot_token].add(grad_back)[:row_count]
    )
    shared_out_grad = jnp.einsum(
        "tf,td->fd", shared_hidden, cotangent, preferred_element_type=single
    )
    grad_shared_hidden = jnp.einsum(
        "td,fd->tf", cotangent, shared_down, preferred_element_type=single
    )
    shared_gate = shared_pre[:, :FS]
    shared_up = shared_pre[:, FS:]
    grad_shared_pre = jnp.concatenate(
        [
            grad_shared_hidden * shared_up * swish_slope(shared_gate),
            grad_shared_hidden * swish(shared_gate),
        ],
        axis=-1,
    ).astype(bfloat)
    shared_in_grad = jnp.einsum(
        "td,tf->df", hidden_two, grad_shared_pre, preferred_element_type=single
    )
    grad_hidden_two = grad_hidden_two + jnp.einsum(
        "tf,df->td", grad_shared_pre, shared_wide, preferred_element_type=single
    )
    grad_hidden_two = grad_hidden_two + jnp.einsum(
        "te,de->td", grad_logits, router_wide, precision=highest
    )
    norm2_grad = jnp.sum(grad_hidden_two * normal_two, axis=0)
    grad_normal_two = grad_hidden_two * gain_two.astype(single)
    grad_residual = grad_output + scale_two * (
        grad_normal_two
        - normal_two * jnp.mean(grad_normal_two * normal_two, axis=-1, keepdims=True)
    )
    grad_residual_low = grad_residual.astype(bfloat)
    out_weight_grad = jnp.einsum(
        "td,te->de", context, grad_residual_low, preferred_element_type=single
    )
    grad_context = jnp.einsum(
        "te,de->td", grad_residual_low, outw_full, preferred_element_type=single
    ).astype(bfloat)
    grad_query_pairs, grad_key_pairs, grad_value_pairs = lax.map(
        partial(pair_backward, visible),
        (
            by_pairs(queries),
            by_pairs(key_heads),
            by_pairs(values),
            log_totals,
            by_pairs(grad_context),
        ),
    )
    grad_query = unrotate(
        from_pairs(grad_query_pairs).reshape(row_count, HEADS, HEAD), cosine, sine_table
    ).reshape(row_count, D)
    grad_key = unrotate(
        from_pairs(grad_key_pairs).reshape(row_count, HEADS, HEAD), cosine, sine_table
    ).reshape(row_count, D)
    grad_projected = jnp.concatenate(
        [grad_query, grad_key, from_pairs(grad_value_pairs)], axis=1
    ).astype(bfloat)
    qkv_grad = jnp.einsum("td,tf->df", hidden_one, grad_projected, preferred_element_type=single)
    grad_hidden_one = jnp.einsum(
        "tf,df->td", grad_projected, qkv_full, preferred_element_type=single
    )
    norm1_grad = jnp.sum(grad_hidden_one * normal_one, axis=0)
    grad_normal_one = grad_hidden_one * gain_one.astype(single)
    input_grad = grad_residual + scale_one * (
        grad_normal_one
        - normal_one * jnp.mean(grad_normal_one * normal_one, axis=-1, keepdims=True)
    )
    summed = (
        lax.psum_scatter(
            norm1_grad.astype(jnp.bfloat16), "dp", scatter_dimension=0, tiled=True
        ).astype(jnp.float32),
        lax.psum_scatter(
            qkv_grad.astype(jnp.bfloat16), "dp", scatter_dimension=0, tiled=True
        ).astype(jnp.float32),
        lax.psum_scatter(
            out_weight_grad.astype(jnp.bfloat16), "dp", scatter_dimension=0, tiled=True
        ).astype(jnp.float32),
        lax.psum_scatter(
            norm2_grad.astype(jnp.bfloat16), "dp", scatter_dimension=0, tiled=True
        ).astype(jnp.float32),
        lax.psum_scatter(
            router_grad.astype(jnp.bfloat16), "dp", scatter_dimension=0, tiled=True
        ).astype(jnp.float32),
        lax.psum_scatter(
            shared_in_grad.astype(jnp.bfloat16), "dp", scatter_dimension=0, tiled=True
        ).astype(jnp.float32),
        lax.psum_scatter(
            shared_out_grad.astype(jnp.bfloat16), "dp", scatter_dimension=0, tiled=True
        ).astype(jnp.float32),
        lax.psum_scatter(
            expert_in_grad.astype(jnp.bfloat16), "dp", scatter_dimension=1, tiled=True
        ).astype(jnp.float32),
        lax.psum_scatter(
            expert_out_grad.astype(jnp.bfloat16), "dp", scatter_dimension=1, tiled=True
        ).astype(jnp.float32),
    )
    dense_sums = (
        lax.psum(summed[0].astype(jnp.bfloat16), "expert").astype(jnp.float32),
        lax.psum(summed[1].astype(jnp.bfloat16), "expert").astype(jnp.float32),
        lax.psum(summed[2].astype(jnp.bfloat16), "expert").astype(jnp.float32),
        lax.psum(summed[3].astype(jnp.bfloat16), "expert").astype(jnp.float32),
        lax.psum(summed[4].astype(jnp.bfloat16), "expert").astype(jnp.float32),
        lax.psum(summed[5].astype(jnp.bfloat16), "expert").astype(jnp.float32),
        lax.psum(summed[6].astype(jnp.bfloat16), "expert").astype(jnp.float32),
    )
    expert_sums = (summed[7], summed[8])
    return (
        output,
        input_grad,
        dense_sums[0],
        dense_sums[1],
        dense_sums[2],
        dense_sums[3],
        dense_sums[4],
        dense_sums[5],
        dense_sums[6],
        expert_sums[0],
        expert_sums[1],
    )


def solution(mesh):
    return jax.shard_map(
        local,
        mesh=mesh,
        in_specs=(
            P(("expert", "dp"), None),
            P(("expert", "dp"), None),
            P(("expert", "dp"), None),
            P(("expert", "dp"), None),
            P(("expert", "dp"), None),
            P("dp"),
            P("dp", None),
            P("dp", None),
            P("dp"),
            P("dp", None),
            P("dp", None),
            P("dp", None),
            P("expert", "dp", None),
            P("expert", "dp", None),
        ),
        out_specs=(
            P(("expert", "dp"), None),
            P(("expert", "dp"), None),
            P("dp"),
            P("dp", None),
            P("dp", None),
            P("dp"),
            P("dp", None),
            P("dp", None),
            P("dp", None),
            P("expert", "dp", None),
            P("expert", "dp", None),
        ),
        check_vma=False,
    )
```

profile of v0, /device:TPU:0, one launch (start us, length us, event | category | flops | bytes accessed | tf_op | source)
XLA Modules:
  0.0 2029.5 jit_solution(8839861436932736356)
XLA Ops:
  13.3 23.6 %all-reduce.6 = (bf16[768]{0:T(1024)(128)(2,1)S(1)}, bf16[768]{0:T(1024)(128)(2,1)S(1)}) all-reduce(bf16[768]{0:T(1024)(128)(2,1)S(1)} %dynamic-update-slice, bf16[768]{0:T(1024)(128)(2,1)S(1)} %dynamic-update-slice.1), channel_id=1, replica_groups=mesh['expert'=4,'dp'=8] {'dp'}, use_global_device_ids=true, to_apply=%add.1 | all-reduce | flops 1536 | bytes 6144
  37.6 40.2 %all-gather.8.cloned.1.call-done = bf16[768,2304]{1,0:T(8,128)(2,1)} async-done(((bf16[96,2304]{1,0:T(8,128)(2,1)}), bf16[768,2304]{1,0:T(8,128)(2,1)}) %all-gather.8.cloned.1.call-update) | async-done | bytes 3538960 | tf_op jit(solution)/shard_map/all_gather | solution.py:135
  84.8 13.1 while.28
  98.0 21.8 %all-gather.10.cloned.1.call-done = bf16[768,768]{1,0:T(8,128)(2,1)} async-done(((bf16[96,768]{1,0:T(8,128)(2,1)}), bf16[768,768]{1,0:T(8,128)(2,1)}) %all-gather.10.cloned.1.call-update) | async-done | bytes 1179664 | tf_op jit(solution)/shard_map/all_gather | solution.py:136
  122.7 96.7 %all-gather.12.cloned.1.call-done = bf16[768,4096]{1,0:T(8,128)(2,1)} async-done(((bf16[96,4096]{1,0:T(8,128)(2,1)}), bf16[768,4096]{1,0:T(8,128)(2,1)}) %all-gather.12.cloned.1.call-update) | async-done | bytes 6291472 | tf_op jit(solution)/shard_map/all_gather | solution.py:139
  226.0 53.7 %all-gather.14.cloned.1.call-done = bf16[2048,768]{1,0:T(8,128)(2,1)} async-done(((bf16[256,768]{1,0:T(8,128)(2,1)}), bf16[2048,768]{1,0:T(8,128)(2,1)}) %all-gather.14.cloned.1.call-update) | async-done | bytes 3145744 | tf_op jit(solution)/shard_map/all_gather | solution.py:140
  321.3 438.8 %all-gather.16.cloned.1.call-done = bf16[4,768,4096]{2,1,0:T(8,128)(2,1)} async-done(((bf16[4,96,4096]{2,1,0:T(8,128)(2,1)}), bf16[4,768,4096]{2,1,0:T(8,128)(2,1)}) %all-gather.16.cloned.1.call-update) | async-done | bytes 25165840 | tf_op jit(solution)/shard_map/all_gather | solution.py:141
  760.2 16.4 fusion.58
  781.4 156.9 %all-gather.18.cloned.1.call-done = bf16[4,2048,768]{2,1,0:T(8,128)(2,1)} async-done(((bf16[4,256,768]{2,1,0:T(8,128)(2,1)}), bf16[4,2048,768]{2,1,0:T(8,128)(2,1)}) %all-gather.18.cloned.1.call-update) | async-done | bytes 12582928 | tf_op jit(solution)/shard_map/all_gather | solution.py:142
  955.2 31.1 %all-gather = bf16[8,96,16]{1,2,0:T(8,128)(2,1)S(1)} all-gather(bf16[1,96,16]{1,2,0:T(8,128)(2,1)S(1)} %bitcast.276), channel_id=1, replica_groups=mesh['expert'=4,'dp'=8] {'dp'}, dimensions={0}, use_global_device_ids=true | all-gather | bytes 27648 | tf_op jit(solution)/shard_map/all_gather | solution.py:138
  1001.7 16.8 all_to_all.20
  1018.5 12.3 fusion.62
  1030.8 14.3 fusion.79
  1049.7 13.6 all-to-all-done.3
  1085.1 46.0 %while.29 = (s32[]{:T(128)}, f32[6,256,2,64]{1,3,2,0:T(8,128)S(1)}, f32[6,256,2,64]{1,3,2,0:T(8,128)}, bf16[6,256,2,64]{1,3,2,0:T(8,128)(2,1)}, bf16[6,256,2,64]...) while((s32[]{:T(128)}, f32[6,256,2,64]{1,3,2,0:T(8,128)S(1)}, ...), condition=%wide.region_24.25_spmd.clone, body=%wide.region_22.24_spmd.clone.sunk | while | flops 85458432 | bytes 4932225 | solution.py:324
  1140.9 64.1 %reduce-scatter.12.cloned.1.call-done = bf16[96,768]{1,0:T(8,128)(2,1)} async-done(((bf16[768,768]{1,0:T(8,128)(2,1)}), bf16[96,768]{1,0:T(8,128)(2,1)}) %reduce-scatter.12.cloned.1.call-update) | async-done | bytes 147472 | tf_op jit(solution)/shard_map/reduce_scatter | solution.py:360
  1205.0 82.0 %reduce-scatter.10.cloned.1.call-done = bf16[96,2304]{1,0:T(8,128)(2,1)} async-done(((bf16[768,2304]{1,0:T(8,128)(2,1)}), bf16[96,2304]{1,0:T(8,128)(2,1)}) %reduce-scatter.10.cloned.1.call-update) | async-done | bytes 442384 | tf_op jit(solution)/shard_map/reduce_scatter | solution.py:357
  1287.1 9.9 bitcast_convert_fusion.1
  1298.2 13.5 bitcast_convert_fusion
  1322.2 30.2 %reduce-scatter.22.cloned.1.call-done = bf16[96,16]{1,0:T(8,128)(2,1)} async-done(((bf16[768,16]{1,0:T(8,128)(2,1)}), bf16[96,16]{1,0:T(8,128)(2,1)}) %reduce-scatter.22.cloned.1.call-update) | async-done | bytes 3088
  1356.8 19.5 all-reduce.5
  1384.9 15.1 all-reduce.11.cloned.1.call-done
  1406.2 205.0 %reduce-scatter.20.cloned.1.call-done = bf16[4,256,768]{2,1,0:T(8,128)(2,1)} async-done(((bf16[4,2048,768]{2,1,0:T(8,128)(2,1)}), bf16[4,256,768]{2,1,0:T(8,128)(2,1)}) %reduce-scatter.20.cloned.1.call-update) | async-done | bytes 1572880 | tf_op jit(solution)/shard_map/reduce_scatter | solution.py:378
  1614.5 402.6 %reduce-scatter.18.cloned.1.call-done = bf16[4,96,4096]{2,1,0:T(8,128)(2,1)} async-done(((bf16[4,768,4096]{2,1,0:T(8,128)(2,1)}), bf16[4,96,4096]{2,1,0:T(8,128)(2,1)}) %reduce-scatter.18.cloned.1.call-update) | async-done | bytes 3145744 | tf_op jit(solution)/shard_map/reduce_scatter | solution.py:375
  (351 shorter events, 234.3 us)
Async XLA Ops:
  7.2 70.6 %all-gather.8.cloned.1.call-start = ((), (), s32[]{:S(2)}) async-start(), calls=%async_computation.11 | async-start | bytes 3981312 | tf_op jit(solution)/shard_map/all_gather | solution.py:135
  8.0 111.9 %all-gather.10.cloned.1.call-start = ((), (), s32[]{:S(2)}) async-start(), calls=%async_computation.12 | async-start | bytes 1327104 | tf_op jit(solution)/shard_map/all_gather | solution.py:136
  8.7 210.7 %all-gather.12.cloned.1.call-start = ((), (), s32[]{:S(2)}) async-start(), calls=%async_computation.13 | async-start | bytes 7077888 | tf_op jit(solution)/shard_map/all_gather | solution.py:139
  9.4 270.2 %all-gather.14.cloned.1.call-start = ((), (), s32[]{:S(2)}) async-start(), calls=%async_computation.14 | async-start | bytes 3538944 | tf_op jit(solution)/shard_map/all_gather | solution.py:140
  10.0 750.1 %all-gather.16.cloned.1.call-start = ((), (), s32[]{:S(2)}) async-start(), calls=%async_computation.15 | async-start | bytes 28311552 | tf_op jit(solution)/shard_map/all_gather | solution.py:141
  10.6 927.7 %all-gather.18.cloned.1.call-start = ((), (), s32[]{:S(2)}) async-start(), calls=%async_computation.16 | async-start | bytes 14155776 | tf_op jit(solution)/shard_map/all_gather | solution.py:142
  11.2 1129.7 %reduce-scatter.16.cloned.1.call-start = ((), (), s32[]{:S(2)}) async-start(), calls=%async_computation.20 | async-start | bytes 3538944 | tf_op jit(solution)/shard_map/reduce_scatter | solution.py:372
  98.0 128.0 %copy-start.7 = (bf16[6,256,2,64]{1,3,2,0:T(8,128)(2,1)}, bf16[6,256,2,64]{1,3,2,0:T(8,128)(2,1)S(1)}, u32[]{:S(2)}) copy-start(bf16[6,256,2,64]{1,3,2,0:T(8,128)(2,1)S(1)} %get-tuple-element.507) | copy-start | bytes 1179652
  98.0 128.0 %copy-start.8 = (bf16[6,256,2,64]{1,3,2,0:T(8,128)(2,1)}, bf16[6,256,2,64]{1,3,2,0:T(8,128)(2,1)S(1)}, u32[]{:S(2)}) copy-start(bf16[6,256,2,64]{1,3,2,0:T(8,128)(2,1)S(1)} %get-tuple-element.508) | copy-start | bytes 1179652
  98.0 128.0 %copy-start.30 = (pred[256]{0:T(512)(128)(4,1)}, pred[256]{0:T(512)(128)(4,1)S(1)}, u32[]{:S(2)}) copy-start(pred[256]{0:T(512)(128)(4,1)S(1)} %get-tuple-element.551) | copy-start | bytes 772
  122.7 157.0 %copy-start.11 = (bf16[256,768]{1,0:T(8,128)(2,1)S(1)}, bf16[256,768]{1,0:T(8,128)(2,1)}, u32[]{:S(2)}) copy-start(bf16[256,768]{1,0:T(8,128)(2,1)} %param.22) | copy-start | bytes 1179652
  304.1 17.2 all-to-all-start
  307.6 833.2 %reduce-scatter.14.cloned.1.call-start = ((), (), s32[]{:S(2)}) async-start(), calls=%async_computation.19 | async-start | bytes 7077888 | tf_op jit(solution)/shard_map/reduce_scatter | solution.py:369
  321.3 438.8 %copy-start.5 = (bf16[4,4,40,768]{3,2,1,0:T(8,128)(2,1)}, bf16[4,4,40,768]{3,2,1,0:T(8,128)(2,1)S(1)}, u32[]{:S(2)}) copy-start(bf16[4,4,40,768]{3,2,1,0:T(8,128)(2,1)S(1)} %all-to-all-done) | copy-start | bytes 2949124
  781.4 163.7 %copy-start.2 = (bf16[4,4,40,2048]{3,2,0,1:T(8,128)(2,1)}, bf16[4,4,40,2048]{3,2,0,1:T(8,128)(2,1)S(1)}, u32[]{:S(2)}) copy-start(bf16[4,4,40,2048]{3,2,0,1:T(8,128)(2,1)S(1)} %multiply_convert_fusion.1) | copy-start | bytes 7864324
  946.2 42.1 %all-to-all-start.1 = ((bf16[4,4,40,768]{3,2,1,0:T(8,128)(2,1)}), bf16[4,4,40,768]{3,2,1,0:T(8,128)(2,1)S(1)}, u32[]{:S(2)}, u32[]{:S(2)}) async-start(bf16[4,4,40,768]{3,2,1,0:T(8,128)(2,1)} %copy.148), calls=%async_computation.1 | async-start | bytes 1966080 | tf_op jit(solution)/shard_map/all_to_all | solution.py:211
  1046.2 17.2 all-to-all-start.3
  1049.7 155.3 %reduce-scatter.12.cloned.1.call-start = ((), (), s32[]{:S(2)}) async-start(), calls=%async_computation.18 | async-start | bytes 1327104 | tf_op jit(solution)/shard_map/reduce_scatter | solution.py:360
  1085.0 202.0 %reduce-scatter.10.cloned.1.call-start = ((), (), s32[]{:S(2)}) async-start(), calls=%async_computation.17 | async-start | bytes 3981312 | tf_op jit(solution)/shard_map/reduce_scatter | solution.py:357
  1137.7 149.3 %copy-start.18 = (bf16[4,4,40,768]{3,2,1,0:T(8,128)(2,1)S(1)}, bf16[4,4,40,768]{3,2,1,0:T(8,128)(2,1)}, u32[]{:S(2)}) copy-start(bf16[4,4,40,768]{3,2,1,0:T(8,128)(2,1)} %copy-done.17) | copy-start | bytes 2949124
  1137.7 214.7 %reduce-scatter.22.cloned.1.call-start = ((), (), s32[]{:S(2)}) async-start(), calls=%async_computation.23 | async-start | bytes 221184
  1140.8 259.3 %all-reduce.11.cloned.1.call-start = ((), (), s32[]{:S(2)}) async-start(), calls=%async_computation.24 | async-start | bytes 3538944 | tf_op jit(solution)/shard_map/psum | solution.py:384
  1287.0 324.2 %reduce-scatter.20.cloned.1.call-start = ((), (), s32[]{:S(2)}) async-start(), calls=%async_computation.22 | async-start | bytes 14155776 | tf_op jit(solution)/shard_map/reduce_scatter | solution.py:378
  1297.0 720.2 %reduce-scatter.18.cloned.1.call-start = ((), (), s32[]{:S(2)}) async-start(), calls=%async_computation.21 | async-start | bytes 28311552 | tf_op jit(solution)/shard_map/reduce_scatter | solution.py:375
  (43 other events, 535.6 us)
Sparse Core Ops, SparseCore 0:
  10.2 67.5 all-gather.7
  79.9 39.8 all-gather.9
  122.0 97.3 all-gather.11
  221.5 58.1 all-gather.13
  281.1 479.0 all-gather.15
  762.2 176.0 all-gather.17
  942.5 73.2 reduce-scatter.15
  1019.9 117.1 reduce-scatter.13
  1141.1 63.8 reduce-scatter.11
  1208.5 78.4 reduce-scatter.9
  1290.8 61.5 reduce-scatter.21
  1354.9 45.1 all-reduce.10
  1403.6 207.5 reduce-scatter.19
  1614.9 402.1 reduce-scatter.17
where the time goes:
time: 2040 us; the launch traced here: 2030 us
  waiting for transfers between devices  1630 us (80%)
  matrix products  172 us (8%)
  blocking collectives  96.7 us (5%)
  other arithmetic  54.8 us (3%)
  local copies, waits for them, and re-layouts  45.3 us (2%)
    all_gather x1, waiting for transfers between devices, local(): lax.all_gather(expert_in, 'dp', axis=1, tiled=True)  439 us
    reduce_scatter x1, waiting for transfers between devices, local(): lax.psum_scatter(expert_in_grad.astype(jnp.bfloat16), 'dp', scatter_dimen...  403 us
    reduce_scatter x1, waiting for transfers between devices, local(): lax.psum_scatter(expert_out_grad.astype(jnp.bfloat16), 'dp', scatter_dime...  205 us
    all_gather x1, waiting for transfers between devices, local(): lax.all_gather(expert_out, 'dp', axis=1, tiled=True)  157 us
    all_gather x1, waiting for transfers between devices, local(): lax.all_gather(shared_in, 'dp', axis=0, tiled=True)  96.7 us
    reduce_scatter x1, waiting for transfers between devices, local(): lax.psum_scatter(qkv_grad.astype(jnp.bfloat16), 'dp', scatter_dimension=0...  82 us
    reduce_scatter x1, waiting for transfers between devices, local(): lax.psum_scatter(out_weight_grad.astype(jnp.bfloat16), 'dp', scatter_dime...  64.1 us
    all_gather x1, waiting for transfers between devices, local(): lax.all_gather(shared_out, 'dp', axis=0, tiled=True)  53.7 us
  transfers between devices with their start and end apart: 17, of which 14 were waited for; matrix products, arithmetic and copies ran while one was open for 13% of the time, Pallas kernels for 0%

commit v1 on v0

v1 whole, which is shorter than its diff:
```python
from functools import partial

import jax
import jax.numpy as jnp
from jax import lax
from jax.sharding import Mesh
from jax.sharding import PartitionSpec as P

D = 768
HEADS = 12
HEAD = 64
EXPERTS = 16
FF = 2048
TOP = 2
FS = 2048
CONTS = 4
TOK_DEV = 256
PROMPT = 128
CAP = 40


epsilon = 1e-06
rope_base = 10000.0
highest = lax.Precision.HIGHEST
bfloat = jnp.bfloat16
single = jnp.float32


def layout(cont_row):
    labels = jnp.arange(CONTS, dtype=jnp.int32)
    member = cont_row[:, None] == labels[None, :]
    lengths = jnp.sum(member.astype(jnp.int32), axis=0)
    starts = jnp.cumsum(lengths) - lengths
    begins = jnp.sum(jnp.where(member, starts[None, :], 0), axis=1)
    offsets = jnp.arange(cont_row.shape[0], dtype=jnp.int32) - begins
    position = jnp.concatenate([jnp.arange(PROMPT, dtype=jnp.int32), PROMPT + offsets])
    segment = jnp.concatenate([jnp.full((PROMPT,), -1, jnp.int32), cont_row])
    rows_at = jnp.arange(TOK_DEV, dtype=jnp.int32)
    visible = (rows_at[None, :] <= rows_at[:, None]) & (segment[None, :] == segment[:, None]) | (
        rows_at[None, :] < PROMPT
    ) & (rows_at[:, None] >= PROMPT)
    half_dim = HEAD // 2
    frequency = rope_base ** (-(jnp.arange(half_dim, dtype=single) * 2.0) / HEAD)
    angles = position.astype(single)[:, None] * frequency[None, :]
    cosine = jnp.concatenate([jnp.cos(angles), jnp.cos(angles)], axis=1)
    sine_table = jnp.concatenate([jnp.sin(angles), jnp.sin(angles)], axis=1)
    return (visible, cosine, sine_table)


def rotate(values, cosine, sine_table):
    half_dim = HEAD // 2
    turned = jnp.concatenate([-values[..., half_dim:], values[..., :half_dim]], axis=-1)
    return values * cosine[:, None, :] + turned * sine_table[:, None, :]


def unrotate(gradient, cosine, sine_table):
    half_dim = HEAD // 2
    turned = jnp.concatenate([gradient[..., half_dim:], -gradient[..., :half_dim]], axis=-1)
    return gradient * cosine[:, None, :] + turned * sine_table[:, None, :]


def swish(gate_part):
    return gate_part * jax.nn.sigmoid(gate_part)


def swish_slope(gate_part):
    sigmoid_value = jax.nn.sigmoid(gate_part)
    return sigmoid_value * (1.0 + gate_part * (1.0 - sigmoid_value))


def slot_plan(route_rows, prio_row):
    expert_of = route_rows.reshape(-1)
    ahead = (expert_of[:, None] == expert_of[None, :]) & (prio_row[None, :] < prio_row[:, None])
    return jnp.sum(ahead.astype(jnp.int32), axis=1).reshape(route_rows.shape)


def flip(value):
    return lax.ppermute(value, "core", [(0, 1), (1, 0)])


def halves(wide, blocks):
    size = wide.shape[-1] // blocks
    half = size // 2
    return tuple(
        jnp.concatenate(
            [wide[..., b * size + c * half : b * size + (c + 1) * half] for b in range(blocks)],
            axis=-1,
        )
        for c in range(2)
    )


def rejoin(first, second, blocks):
    half = first.shape[-1] // blocks
    pieces = []
    for b in range(blocks):
        pieces += [first[..., b * half : (b + 1) * half], second[..., b * half : (b + 1) * half]]
    return jnp.concatenate(pieces, axis=-1)


def pair_forward(visible, pieces):
    query_pair, key_pair, value_pair = pieces
    scores = jnp.einsum("qhd,khd->hqk", query_pair, key_pair, preferred_element_type=single) * 0.125
    scores = jnp.where(visible[None], scores, -1e30)
    top_score = jnp.max(scores, axis=-1, keepdims=True)
    weights = jnp.exp(scores - top_score)
    totals = jnp.sum(weights, axis=-1, keepdims=True)
    attention = (weights / totals).astype(bfloat)
    context = jnp.einsum("hqk,khd->qhd", attention, value_pair, preferred_element_type=single)
    return (context.astype(bfloat), (top_score + jnp.log(totals))[..., 0])


def pair_backward(visible, pieces):
    query_pair, key_pair, value_pair, log_total, grad_context = pieces
    scores = jnp.einsum("qhd,khd->hqk", query_pair, key_pair, preferred_element_type=single) * 0.125
    scores = jnp.where(visible[None], scores, -1e30)
    attention = jnp.exp(scores - log_total[..., None])
    attention_low = attention.astype(bfloat)
    grad_value = jnp.einsum(
        "hqk,qhd->khd", attention_low, grad_context, preferred_element_type=single
    )
    grad_attention = jnp.einsum(
        "qhd,khd->hqk", grad_context, value_pair, preferred_element_type=single
    )
    grad_scores = (
        attention * (grad_attention - jnp.sum(attention * grad_attention, axis=-1, keepdims=True))
    ).astype(bfloat)
    grad_query = (
        jnp.einsum("hqk,khd->qhd", grad_scores, key_pair, preferred_element_type=single) * 0.125
    )
    grad_key = (
        jnp.einsum("hqk,qhd->khd", grad_scores, query_pair, preferred_element_type=single) * 0.125
    )
    return (grad_query, grad_key, grad_value)


CHIPS = ("r", "j", "x")
DEVICES = ("r", "j", "x", "core")
PEERS = ("x", "core")
ROWS = ("r", "j")
OWNERS = ("x", "core", "j")


def swiglu(pre, width):
    return (swish(pre[:, :width]) * pre[:, width:]).astype(bfloat)


def swiglu_back(grad, pre, width):
    gate, up = pre[:, :width], pre[:, width:]
    return jnp.concatenate([grad * up * swish_slope(gate), grad * swish(gate)], axis=-1).astype(
        bfloat
    )


def dot(left, right, left_axis=1, right_axis=0):
    return lax.dot_general(
        left, right, (((left_axis,), (right_axis,)), ((), ())), preferred_element_type=single
    )


def local(
    layer_input,
    routes,
    priority,
    cont_ids,
    cotangent,
    norm1_gain,
    qkv_weight,
    out_weight,
    norm2_gain,
    router_weight,
    shared_in,
    shared_out,
    expert_in,
    expert_out,
):
    row_count = layer_input.shape[0]
    spans_x = lax.axis_size("x")
    owners = lax.axis_size("j")
    copies = lax.axis_size("r")
    shards = copies * owners
    core = lax.axis_index("core")
    x_at = lax.axis_index("x")
    first_core = core == 0
    half_ff = FF // 2
    half_fs = FS // 2
    shard_rows = D // shards
    block = FF // shards

    def mine_of(pair):
        return jnp.where(first_core, pair[0], pair[1])

    def other_of(pair):
        return jnp.where(first_core, pair[1], pair[0])

    def part(rows, index, count):
        size = rows.shape[0] // count
        return lax.dynamic_slice_in_dim(rows, index * size, size, 0)

    packed = jnp.concatenate(
        [
            qkv_weight,
            norm1_gain[:, None],
            norm2_gain[:, None],
            router_weight,
            jnp.zeros((shard_rows, 110), bfloat),
        ],
        axis=1,
    )
    peer = x_at * 2 + core
    packed_full = lax.all_gather(part(packed, peer, spans_x * 2), DEVICES, axis=0, tiled=True)
    outw_full = lax.all_gather(part(out_weight, peer, spans_x * 2), DEVICES, axis=0, tiled=True)
    shared_wide = lax.all_gather(
        mine_of(halves(part(shared_in, x_at, spans_x), 2 * shards)), CHIPS, axis=0, tiled=True
    )
    shared_down = lax.all_gather(
        part(part(shared_out, core, 2), x_at, spans_x), CHIPS, axis=0, tiled=True
    )
    qkv_full = packed_full[:, : 3 * D]
    gain_one = packed_full[:, 3 * D].astype(single)
    gain_two = packed_full[:, 3 * D + 1].astype(single)
    router_full = packed_full[:, 3 * D + 2 : 3 * D + 2 + EXPERTS]

    in_pair = halves(expert_in, 2 * shards)
    out_pair = (expert_out[:, : block // 2], expert_out[:, block // 2 :])

    def to_owner(pair):
        mine, other = mine_of(pair), flip(other_of(pair))
        whole = jnp.where(
            first_core, jnp.concatenate([mine, other]), jnp.concatenate([other, mine])
        )
        whole = jnp.tile(whole, (copies, 1, 1))
        return lax.all_to_all(whole, ROWS, split_axis=0, concat_axis=0, tiled=True)

    expert_wide = to_owner(in_pair).reshape(D, 2 * half_ff)
    expert_down = to_owner(out_pair).reshape(half_ff, D)

    visible, cosine, sine_table = layout(cont_ids[0])

    def by_pairs(stacked):
        return jnp.moveaxis(stacked.reshape(row_count, HEADS // 2, 2, HEAD), 1, 0)

    def from_pairs(stacked):
        return jnp.moveaxis(stacked, 0, 1).reshape(row_count, D)

    inputs = layer_input.astype(single)
    scale_one = lax.rsqrt(jnp.mean(inputs * inputs, axis=-1, keepdims=True) + epsilon)
    normal_one = inputs * scale_one
    hidden_one = (normal_one * gain_one).astype(bfloat)
    projected = dot(hidden_one, qkv_full)
    queries = rotate(projected[:, :D].reshape(row_count, HEADS, HEAD), cosine, sine_table).astype(
        bfloat
    )
    key_heads = rotate(
        projected[:, D : 2 * D].reshape(row_count, HEADS, HEAD), cosine, sine_table
    ).astype(bfloat)
    values = projected[:, 2 * D :].astype(bfloat)
    context_pairs, log_totals = lax.map(
        partial(pair_forward, visible), (by_pairs(queries), by_pairs(key_heads), by_pairs(values))
    )
    context = from_pairs(context_pairs)
    residual = inputs + dot(context, outw_full)
    scale_two = lax.rsqrt(jnp.mean(residual * residual, axis=-1, keepdims=True) + epsilon)
    normal_two = residual * scale_two
    hidden_two = (normal_two * gain_two).astype(bfloat)
    gate_probs = jax.nn.softmax(dot(hidden_two, router_full), axis=-1)

    slot_index = slot_plan(routes, priority[0])
    spot = ((routes // owners) * 2 * owners + routes % owners) * CAP + slot_index
    spot = jnp.where(slot_index < CAP, spot, -1)
    exchange = spans_x * 2 * owners * CAP
    places = jnp.arange(exchange, dtype=jnp.int32)
    shift = owners * CAP
    takes = [
        (places[:, None] == spot[None, :, k]) for k in range(TOP)
    ]
    pair_gate = jnp.take_along_axis(gate_probs, routes, axis=1)
    token_pick = (takes[0] | takes[1]).astype(bfloat).reshape(spans_x, 2, shift, row_count)[:, 0]
    token_pick = token_pick.reshape(spans_x * shift, row_count)
    slot_gate = sum(
        jnp.sum(
            jnp.where(takes[k].reshape(spans_x, 2, shift, row_count)[:, 0], pair_gate[:, k], 0.0),
            axis=-1,
        )
        for k in range(TOP)
    ).reshape(spans_x * shift, 1)
    slot_hidden = dot(token_pick, hidden_two).astype(bfloat)
    slot_grad = (slot_gate * dot(token_pick, cotangent)).astype(bfloat)
    outgoing = jnp.stack(
        [slot_hidden.reshape(spans_x, shift, D), slot_grad.reshape(spans_x, shift, D)], axis=1
    ).reshape(exchange, D)
    arrived = lax.all_to_all(outgoing, OWNERS, split_axis=0, concat_axis=0, tiled=True)

    pair_hidden = jnp.concatenate([hidden_two, flip(hidden_two)])
    pair_cotangent = jnp.concatenate([cotangent, flip(cotangent)])
    shared_pre = dot(pair_hidden, shared_wide)
    shared_hidden = swiglu(shared_pre, half_fs)
    shared_part = dot(shared_hidden, shared_down)
    shared_part = shared_part[:row_count] + flip(shared_part[row_count:].astype(bfloat)).astype(
        single
    )
    shared_out_grad = dot(shared_hidden, pair_cotangent, 0, 0).astype(bfloat)
    grad_shared_pre = swiglu_back(dot(pair_cotangent, shared_down, 1, 1), shared_pre, half_fs)
    shared_in_grad = dot(pair_hidden, grad_shared_pre, 0, 0).astype(bfloat)
    grad_shared = dot(grad_shared_pre, shared_wide, 1, 1)
    grad_shared = grad_shared[:row_count] + flip(grad_shared[row_count:].astype(bfloat)).astype(
        single
    )
    shared_in_sum = lax.psum_scatter(shared_in_grad, CHIPS, scatter_dimension=0, tiled=True)
    shared_out_sum = lax.psum_scatter(shared_out_grad, CHIPS, scatter_dimension=0, tiled=True)
    shared_in_sum = lax.all_gather(shared_in_sum, PEERS, axis=0, tiled=False)
    shared_in_sum = shared_in_sum.reshape(spans_x, 2, shard_rows // spans_x, FS)
    shared_in_sum = rejoin(
        shared_in_sum[:, 0].reshape(shard_rows, FS),
        shared_in_sum[:, 1].reshape(shard_rows, FS),
        2 * shards,
    ).astype(single)
    shared_out_sum = lax.all_gather(shared_out_sum, PEERS, axis=0, tiled=False)
    shared_out_sum = (
        jnp.moveaxis(shared_out_sum.reshape(spans_x, 2, -1, D), 1, 0).reshape(FS // shards, D)
    ).astype(single)

    crossed = flip(arrived)
    buffer = jnp.where(first_core, arrived, crossed)
    grad_buffer = jnp.where(first_core, crossed, arrived)
    expert_pre = dot(buffer, expert_wide)
    expert_hidden = swiglu(expert_pre, half_ff)
    expert_result = dot(expert_hidden, expert_down)
    grad_expert_pre = swiglu_back(dot(grad_buffer, expert_down, 1, 1), expert_pre, half_ff)
    grad_rows = dot(grad_expert_pre, expert_wide, 1, 1)
    kept = jnp.where(first_core, expert_result, grad_rows)
    given = jnp.where(first_core, grad_rows, expert_result).astype(bfloat)
    finished = (kept + flip(given).astype(single)).astype(bfloat)
    returned = lax.all_to_all(finished, OWNERS, split_axis=0, concat_axis=0, tiled=True)

    expert_out_grad = dot(expert_hidden, grad_buffer, 0, 0).astype(bfloat)
    expert_in_grad = dot(buffer, grad_expert_pre, 0, 0).astype(bfloat)

    def to_shards(grads):
        spread = lax.all_to_all(grads, ROWS, split_axis=0, concat_axis=0, tiled=True)
        spread = spread.reshape((copies, owners) + spread.shape[1:])
        if copies > 1:
            spread = jnp.sum(spread.astype(single), axis=0).astype(bfloat)
        else:
            spread = spread[0]
        low, high = spread[: owners // 2], spread[owners // 2 :]
        mine = jnp.where(first_core, low, high)
        other = flip(jnp.where(first_core, high, low))
        return (jnp.where(first_core, mine, other), jnp.where(first_core, other, mine))

    expert_in_sum = rejoin(
        *to_shards(expert_in_grad.reshape(shards, shard_rows, 2 * half_ff)), 2 * shards
    ).astype(single)
    expert_out_sum = jnp.concatenate(
        to_shards(expert_out_grad.reshape(shards, block // 2, D)), axis=1
    ).astype(single)

    result_picks = [(spot[:, k, None] == places[None, :]).astype(bfloat) for k in range(TOP)]
    pair_results = [dot(pick, returned) for pick in result_picks]
    routed = sum(pair_gate[:, k, None] * pair_results[k] for k in range(TOP))
    output = (residual + shared_part + routed).astype(bfloat)
    grad_output = cotangent.astype(single)
    expert_ids = jnp.arange(EXPERTS, dtype=jnp.int32)
    grad_gates = sum(
        jnp.where(
            routes[:, k, None] == expert_ids[None, :],
            jnp.sum(grad_output * pair_results[k], axis=-1, keepdims=True),
            0.0,
        )
        for k in range(TOP)
    )
    grad_logits = gate_probs * (
        grad_gates - jnp.sum(gate_probs * grad_gates, axis=-1, keepdims=True)
    )
    router_grad = jnp.einsum(
        "td,te->de", hidden_two.astype(single), grad_logits, precision=highest
    )
    back_spot = jnp.where(spot >= 0, spot + shift, -1)
    back_pick = (
        (back_spot[:, 0, None] == places[None, :]) | (back_spot[:, 1, None] == places[None, :])
    ).astype(bfloat)
    grad_hidden_two = dot(back_pick, returned) + grad_shared
    grad_hidden_two = grad_hidden_two + jnp.einsum(
        "te,de->td", grad_logits, router_full.astype(single), precision=highest
    )
    norm2_grad = jnp.sum(grad_hidden_two * normal_two, axis=0)
    grad_normal_two = grad_hidden_two * gain_two
    grad_residual = grad_output + scale_two * (
        grad_normal_two
        - normal_two * jnp.mean(grad_normal_two * normal_two, axis=-1, keepdims=True)
    )
    grad_residual_low = grad_residual.astype(bfloat)
    out_weight_grad = dot(context, grad_residual_low, 0, 0).astype(bfloat)
    grad_context = dot(grad_residual_low, outw_full, 1, 1).astype(bfloat)
    grad_query_pairs, grad_key_pairs, grad_value_pairs = lax.map(
        partial(pair_backward, visible),
        (
            by_pairs(queries),
            by_pairs(key_heads),
            by_pairs(values),
            log_totals,
            by_pairs(grad_context),
        ),
    )
    grad_query = unrotate(
        from_pairs(grad_query_pairs).reshape(row_count, HEADS, HEAD), cosine, sine_table
    ).reshape(row_count, D)
    grad_key = unrotate(
        from_pairs(grad_key_pairs).reshape(row_count, HEADS, HEAD), cosine, sine_table
    ).reshape(row_count, D)
    grad_projected = jnp.concatenate(
        [grad_query, grad_key, from_pairs(grad_value_pairs)], axis=1
    ).astype(bfloat)
    qkv_grad = dot(hidden_one, grad_projected, 0, 0).astype(bfloat)
    grad_hidden_one = dot(grad_projected, qkv_full, 1, 1)
    norm1_grad = jnp.sum(grad_hidden_one * normal_one, axis=0)
    grad_normal_one = grad_hidden_one * gain_one
    input_grad = grad_residual + scale_one * (
        grad_normal_one
        - normal_one * jnp.mean(grad_normal_one * normal_one, axis=-1, keepdims=True)
    )

    def reduce_rows(grads):
        summed = lax.psum_scatter(grads, DEVICES, scatter_dimension=0, tiled=True)
        return lax.all_gather(summed, PEERS, axis=0, tiled=True).astype(single)

    outw_sum = reduce_rows(out_weight_grad)
    packed_sum = reduce_rows(
        jnp.concatenate(
            [
                qkv_grad,
                norm1_grad[:, None].astype(bfloat),
                norm2_grad[:, None].astype(bfloat),
                router_grad.astype(bfloat),
                jnp.zeros((D, 110), bfloat),
            ],
            axis=1,
        )
    )
    return (
        output,
        input_grad,
        packed_sum[:, 3 * D],
        packed_sum[:, : 3 * D],
        outw_sum,
        packed_sum[:, 3 * D + 1],
        packed_sum[:, 3 * D + 2 : 3 * D + 2 + EXPERTS],
        shared_in_sum,
        shared_out_sum,
        expert_in_sum,
        expert_out_sum,
    )


def solution(mesh):
    spans_x = mesh.shape["expert"] // 2
    owners = EXPERTS // spans_x
    view = Mesh(
        mesh.devices.reshape(spans_x, 2, mesh.shape["dp"] // owners, owners),
        ("x", "core", "r", "j"),
    )
    tokens = P(("x", "core", "r", "j"), None)
    vector = P(("r", "j"))
    rows = P(("r", "j"), None)
    experts = P(("x", "core"), ("r", "j"), None)
    return jax.shard_map(
        local,
        mesh=view,
        in_specs=(
            (tokens,) * 5
            + (vector, rows, rows, vector, rows, rows, rows, experts, experts)
        ),
        out_specs=(tokens, tokens, vector, rows, rows, vector, rows, rows, rows, experts, experts),
        check_vma=False,
    )
```

time: 2040 us -> 1050 us (0.51)
  waiting for transfers between devices: 1630 us -> 636 us
  local copies, waits for them, and re-layouts: 45.3 us -> 115 us
  blocking collectives: 96.7 us -> 28.9 us
    all_gather x6 -> x4, waiting for transfers between devices: 808 us -> 145 us  [the longest x1 85.7 us: local(): lax.all_gather(part(part(shared_out, core, 2), x_at, spans_x), CHIPS, axi...]
    reduce_scatter x6 -> x3, waiting for transfers between devices: 754 us -> 269 us  [the longest x1 114 us: local(): lax.psum_scatter(shared_out_grad, CHIPS, scatter_dimension=0, tiled=True)]
    all_to_all x3 -> x6, waiting for transfers between devices: 21.2 us -> 123 us  [the longest x2 53.1 us: to_shards(): lax.all_to_all(grads, ROWS, split_axis=0, concat_axis=0, tiled=True)]
    unnamed x111 -> x287, local copies, waits for them, and re-layouts: 8.8 us -> 73.1 us
    unnamed x15 -> x9, waiting for transfers between devices: 34 us -> 93.7 us
    unnamed x2 -> x0, blocking collectives: 43.1 us -> none
    dot_general x21 -> x26, matrix products: 123 us -> 101 us  [the longest x24 98.3 us: dot(): lax.dot_general(left, right, (((left_axis,), (right_axis,)), ((), ())), p...]
  transfers between devices with their start and end apart: 17 -> 24, of which waited for: 14 -> 14; matrix products, arithmetic and copies ran while one was open for 13% -> 30% of each run, Pallas kernels for 0% -> 0%
where the time goes in v1:
time: 1050 us; the launch traced here: 1030 us
  waiting for transfers between devices  636 us (61%)
  matrix products  157 us (15%)
  local copies, waits for them, and re-layouts  115 us (11%)
  other arithmetic  51.6 us (5%)
  starting transfers between devices  29 us (3%)
  blocking collectives  28.9 us (3%)
  between operations  16 us (2%)
    reduce_scatter x1, waiting for transfers between devices, local(): lax.psum_scatter(shared_out_grad, CHIPS, scatter_dimension=0, tiled=True)  114 us
    dot_general x24, matrix products, dot(): lax.dot_general(left, right, (((left_axis,), (right_axis,)), ((), ())), p...  98.3 us
    reduce_scatter x1, waiting for transfers between devices, local(): lax.psum_scatter(shared_in_grad, CHIPS, scatter_dimension=0, tiled=True)  94.4 us
    unnamed x9, waiting for transfers between devices  93.7 us
    all_gather x1, waiting for transfers between devices, local(): lax.all_gather(part(part(shared_out, core, 2), x_at, spans_x), CHIPS, axi...  85.7 us
    unnamed x287, local copies, waits for them, and re-layouts  73.1 us
    reduce_scatter x1, waiting for transfers between devices, reduce_rows(): summed = lax.psum_scatter(grads, DEVICES, scatter_dimension=0, tiled=True)  60.9 us
    all_to_all x2, waiting for transfers between devices, to_shards(): lax.all_to_all(grads, ROWS, split_axis=0, concat_axis=0, tiled=True)  53.1 us
  transfers between devices with their start and end apart: 24, of which 14 were waited for; matrix products, arithmetic and copies ran while one was open for 30% of the time, Pallas kernels for 0%

profile of v1, /device:TPU:0, one launch (start us, length us, event | category | flops | bytes accessed | tf_op | source)
XLA Modules:
  0.0 1033.9 jit_solution(11995306753343150382)
XLA Ops:
  49.9 25.1 %all-gather.7.cloned.1.call-done = bf16[768,2432]{1,0:T(8,128)(2,1)} async-done(((bf16[24,2432]{1,0:T(8,128)(2,1)}), bf16[768,2432]{1,0:T(8,128)(2,1)}) %all-gather.7.cloned.1.call-update) | async-done | bytes 3735568 | tf_op jit(solution)/shard_map/all_gather | solution.py:211
  85.6 16.9 %while.28 = (s32[]{:T(128)}, bf16[6,256,2,64]{1,3,2,0:T(8,128)(2,1)}, f32[6,2,256]{2,1,0:T(2,128)}, bf16[6,256,2,64]{1,3,2,0:T(8,128)(2,1)}, bf16[6,256,2,64]{1,...) while((s32[]{:T(128)}, ...), condition=%wide.region_7.8_spmd.clone, body=%wide.region_4.7_spmd.clone.sunk | while | flops 34962944 | bytes 1986161 | solution.py:258
  102.5 28.0 %all-gather.9.cloned.1.call-done = bf16[768,768]{1,0:T(8,128)(2,1)} async-done(((bf16[24,768]{1,0:T(8,128)(2,1)}), bf16[768,768]{1,0:T(8,128)(2,1)}) %all-gather.9.cloned.1.call-update) | async-done | bytes 1179664 | tf_op jit(solution)/shard_map/all_gather | solution.py:212
  166.3 42.5 %all-to-all-done = bf16[32,40,768]{2,1,0:T(8,128)(2,1)} async-done(((bf16[32,40,768]{2,1,0:T(8,128)(2,1)}), bf16[32,40,768]{2,1,0:T(8,128)(2,1)}, u32[]{:S(2)}, u32[]{:S(2)}) %all-to-all-start) | async-done | bytes 1966112 | tf_op jit(solution)/shard_map/all_to_all | solution.py:292
  216.9 5.8 all-gather.11.cloned.1.call-done
  222.7 5.8 fusion.99
  228.5 85.7 %all-gather.13.cloned.1.call-done = bf16[1024,768]{1,0:T(8,128)(2,1)} async-done(((bf16[64,768]{1,0:T(8,128)(2,1)}), bf16[1024,768]{1,0:T(8,128)(2,1)}) %all-gather.13.cloned.1.call-update) | async-done | bytes 1572880 | tf_op jit(solution)/shard_map/all_gather | solution.py:216
  314.2 5.7 multiply_convert_fusion.5
  348.0 113.9 %reduce-scatter.11.cloned.1.call-done = bf16[64,768]{1,0:T(8,128)(2,1)} async-done(((bf16[1024,768]{1,0:T(8,128)(2,1)}), bf16[64,768]{1,0:T(8,128)(2,1)}) %reduce-scatter.11.cloned.1.call-update) | async-done | bytes 98320 | tf_op jit(solution)/shard_map/reduce_scatter | solution.py:310
  461.9 7.1 all-gather.1
  470.0 10.7 %fusion.93 = f32[1280,2048]{1,0:T(8,128)} fusion(bf16[768,2048]{1,0:T(8,128)(2,1)} %bitcast.30, bf16[1280,768]{1,0:T(8,128)(2,1)} %bitcast.29, bf16[1280,768]{1,0:T(8,128)(2,1)} %collective-permute-done.2, pred[]{:T(512)S(6)} %eq.195), kind=kOutput, calls=%fused_computation.170 | convolution fusion | flops 4027514880 | bytes 17563648 | tf_op jit(solution)/shard_map/dot_general | solution.py:156
  480.7 9.1 multiply_convert_fusion.2
  489.8 5.9 convolution_convert_fusion.5
  504.3 9.4 select_convert_fusion
  513.9 7.6 convolution_convert_fusion.3
  521.4 94.4 %reduce-scatter.9.cloned.1.call-done = bf16[48,2048]{1,0:T(8,128)(2,1)} async-done(((bf16[768,2048]{1,0:T(8,128)(2,1)}), bf16[48,2048]{1,0:T(8,128)(2,1)}) %reduce-scatter.9.cloned.1.call-update) | async-done | bytes 196624 | tf_op jit(solution)/shard_map/reduce_scatter | solution.py:309
  615.8 9.1 all-gather
  648.1 53.1 %all-to-all-done.4 = bf16[8,96,2048]{2,1,0:T(8,128)(2,1)S(1)} async-done(((bf16[8,96,2048]{2,1,0:T(8,128)(2,1)}), bf16[8,96,2048]{2,1,0:T(8,128)(2,1)S(1)}, u32[]{:S(2)}, u32[]{:S(2)}) %all-to-all-start.4) | async-done | bytes 3145760 | tf_op jit(solution)/shard_map/all_to_all | solution.py:340
  724.8 27.1 %all-to-all-done.3 = bf16[32,40,768]{2,1,0:T(8,128)(2,1)} async-done(((bf16[32,40,768]{2,1,0:T(8,128)(2,1)}), bf16[32,40,768]{2,1,0:T(8,128)(2,1)}, u32[]{:S(2)}, u32[]{:S(2)}) %all-to-all-start.3) | async-done | bytes 1966112 | tf_op jit(solution)/shard_map/all_to_all | solution.py:334
  768.6 54.0 %while.29 = (s32[]{:T(128)}, f32[6,256,2,64]{1,3,2,0:T(8,128)}, f32[6,256,2,64]{1,3,2,0:T(8,128)}, bf16[6,256,2,64]{1,3,2,0:T(8,128)(2,1)}, bf16[6,256,2,64]{1,3...) while((s32[]{:T(128)}, f32[6,256,2,64]{1,3,2,0:T(8,128)}, ...), condition=%wide.region_20.21_spmd.clone, body=%wide.region_18.20_spmd.clone.sunk | while | flops 85458432 | bytes 4932233 | solution.py:395
  839.4 6.7 concatenate.121
  856.5 60.9 %reduce-scatter.7.cloned.1.call-done = bf16[24,768]{1,0:T(8,128)(2,1)} async-done(((bf16[768,768]{1,0:T(8,128)(2,1)}), bf16[24,768]{1,0:T(8,128)(2,1)}) %reduce-scatter.7.cloned.1.call-update) | async-done | bytes 36880 | tf_op jit(solution)/shard_map/reduce_scatter | solution.py:424
  923.8 93.5 %reduce-scatter.13.cloned.1.call-done = bf16[24,2432]{1,0:T(8,128)(2,1)} async-done(((bf16[768,2432]{1,0:T(8,128)(2,1)}), bf16[24,2432]{1,0:T(8,128)(2,1)}) %reduce-scatter.13.cloned.1.call-update) | async-done | bytes 116752
  1017.3 7.0 all_gather.34
  (536 shorter events, 303.5 us)
Async XLA Ops:
  7.2 67.8 %all-gather.7.cloned.1.call-start = ((), (), s32[]{:S(2)}) async-start(), calls=%async_computation.10 | async-start | bytes 3852288 | tf_op jit(solution)/shard_map/all_gather | solution.py:211
  11.5 119.0 %all-gather.9.cloned.1.call-start = ((), (), s32[]{:S(2)}) async-start(), calls=%async_computation.11 | async-start | bytes 1216512 | tf_op jit(solution)/shard_map/all_gather | solution.py:212
  13.0 209.7 %all-gather.11.cloned.1.call-start = ((), (), s32[]{:S(2)}) async-start(), calls=%async_computation.12 | async-start | bytes 3342336 | tf_op jit(solution)/shard_map/all_gather | solution.py:213
  142.8 66.0 %all-to-all-start = ((bf16[32,40,768]{2,1,0:T(8,128)(2,1)}), bf16[32,40,768]{2,1,0:T(8,128)(2,1)}, u32[]{:S(2)}, u32[]{:S(2)}) async-start(bf16[32,40,768]{2,1,0:T(8,128)(2,1)} %bitcast.28), calls=%async_computation | async-start | bytes 3932160 | tf_op jit(solution)/shard_map/all_to_all | solution.py:292
  146.4 167.8 %all-gather.13.cloned.1.call-start = ((), (), s32[]{:S(2)}) async-start(), calls=%async_computation.13 | async-start | bytes 1671168 | tf_op jit(solution)/shard_map/all_gather | solution.py:216
  159.3 3.8 collective-permute-start.3
  208.7 119.6 %all-to-all-start.1 = ((bf16[8,96,2048]{2,1,0:T(8,128)(2,1)}), bf16[8,96,2048]{2,1,0:T(8,128)(2,1)}, u32[]{:S(2)}, u32[]{:S(2)}) async-start(bf16[8,96,2048]{2,1,0:T(8,128)(2,1)} %maximum_select_fusion), calls=%async_computation.1 | async-start | bytes 6291456 | tf_op jit(solution)/shard_map/all_to_all | solution.py:233
  213.5 248.4 %reduce-scatter.11.cloned.1.call-start = ((), (), s32[]{:S(2)}) async-start(), calls=%async_computation.16 | async-start | bytes 1671168 | tf_op jit(solution)/shard_map/reduce_scatter | solution.py:310
  213.8 3.1 collective-permute-start.6
  215.6 7.1 collective-permute-start
  324.6 2.4 collective-permute-start.4
  324.7 145.2 %collective-permute-start.2 = (bf16[1280,768]{1,0:T(8,128)(2,1)}, bf16[1280,768]{1,0:T(8,128)(2,1)}, u32[]{:S(2)}, u32[]{:S(2)}) collective-permute-start(bf16[1280,768]{1,0:T(8,128)(2,1)} %bitcast.29), channel_id=1, source_target_pairs={{0,8},{8,0},{1,9},{9,1},{2,10},{10,2},{3,11},{11,3},{4,12},{12,4},... | collective-permute-start | bytes 5898248 | tf_op jit(solution)/shard_map/ppermute | solution.py:78
  328.4 152.3 %all-to-all-start.2 = ((bf16[8,128,768]{2,1,0:T(8,128)(2,1)}), bf16[8,128,768]{2,1,0:T(8,128)(2,1)S(1)}, u32[]{:S(2)}, u32[]{:S(2)}) async-start(bf16[8,128,768]{2,1,0:T(8,128)(2,1)} %maximum_select_fusion.1), calls=%async_computation.2 | async-start | bytes 3145728 | tf_op jit(solution)/shard_map/all_to_all | solution.py:233
  332.8 283.1 %reduce-scatter.9.cloned.1.call-start = ((), (), s32[]{:S(2)}) async-start(), calls=%async_computation.15 | async-start | bytes 3342336 | tf_op jit(solution)/shard_map/reduce_scatter | solution.py:309
  338.7 415.8 %collective-permute-start.1 = (bf16[256,768]{1,0:T(8,128)(2,1)}, bf16[256,768]{1,0:T(8,128)(2,1)}, u32[]{:S(2)}, u32[]{:S(2)}) collective-permute-start(bf16[256,768]{1,0:T(8,128)(2,1)} %slice.996), channel_id=1, source_target_pairs={{0,8},{8,0},{1,9},{9,1},{2,10},{10,2},{3,11},{11,3},{4,12},{12,4},... | collective-permute-start | bytes 1179656 | tf_op jit(solution)/shard_map/ppermute | solution.py:78
  347.6 412.0 %collective-permute-start.7 = (bf16[256,768]{1,0:T(8,128)(2,1)}, bf16[256,768]{1,0:T(8,128)(2,1)}, u32[]{:S(2)}, u32[]{:S(2)}) collective-permute-start(bf16[256,768]{1,0:T(8,128)(2,1)} %slice.995), channel_id=1, source_target_pairs={{0,8},{8,0},{1,9},{9,1},{2,10},{10,2},{3,11},{11,3},{4,12},{12,4},... | collective-permute-start | bytes 1179656 | tf_op jit(solution)/shard_map/ppermute | solution.py:78
  495.7 129.3 %all-to-all-start.5 = ((bf16[8,128,768]{2,1,0:T(8,128)(2,1)}), bf16[8,128,768]{2,1,0:T(8,128)(2,1)S(1)}, u32[]{:S(2)}, u32[]{:S(2)}) async-start(bf16[8,128,768]{2,1,0:T(8,128)(2,1)} %bitcast.235), calls=%async_computation.8 | async-start | bytes 3145728 | tf_op jit(solution)/shard_map/all_to_all | solution.py:340
  513.7 129.7 %collective-permute-start.5 = (bf16[1280,768]{1,0:T(8,128)(2,1)}, bf16[1280,768]{1,0:T(8,128)(2,1)}, u32[]{:S(2)}, u32[]{:S(2)}) collective-permute-start(bf16[1280,768]{1,0:T(8,128)(2,1)} %get-tuple-element.393), channel_id=1, source_target_pairs={{0,8},{8,0},{1,9},{9,1},{2,10},{10,2},{3,11},{11,3},{4,12},{12,4},... | collective-permute-start | bytes 5898248 | tf_op jit(solution)/shard_map/ppermute | solution.py:78
  626.1 75.1 %all-to-all-start.4 = ((bf16[8,96,2048]{2,1,0:T(8,128)(2,1)}), bf16[8,96,2048]{2,1,0:T(8,128)(2,1)S(1)}, u32[]{:S(2)}, u32[]{:S(2)}) async-start(bf16[8,96,2048]{2,1,0:T(8,128)(2,1)} %bitcast.227), calls=%async_computation.7 | async-start | bytes 6291456 | tf_op jit(solution)/shard_map/all_to_all | solution.py:340
  701.2 50.7 %all-to-all-start.3 = ((bf16[32,40,768]{2,1,0:T(8,128)(2,1)}), bf16[32,40,768]{2,1,0:T(8,128)(2,1)}, u32[]{:S(2)}, u32[]{:S(2)}) async-start(bf16[32,40,768]{2,1,0:T(8,128)(2,1)} %bitcast.220), calls=%async_computation.3 | async-start | bytes 3932160 | tf_op jit(solution)/shard_map/all_to_all | solution.py:334
  704.7 212.7 %reduce-scatter.7.cloned.1.call-start = ((), (), s32[]{:S(2)}) async-start(), calls=%async_computation.14 | async-start | bytes 1216512 | tf_op jit(solution)/shard_map/reduce_scatter | solution.py:424
  714.4 6.6 collective-permute-start.9
  724.4 125.2 %collective-permute-start.8 = (bf16[4,96,2048]{2,1,0:T(8,128)(2,1)}, bf16[4,96,2048]{2,1,0:T(8,128)(2,1)}, u32[]{:S(2)}, u32[]{:S(2)}) collective-permute-start(bf16[4,96,2048]{2,1,0:T(8,128)(2,1)} %broadcast_select_fusion.4), channel_id=1, source_target_pairs={{0,8},{8,0},{1,9},{9,1},{2,10},{10,2},{3,11},{11,3},{4,12},{12,4},... | collective-permute-start | bytes 4718600 | tf_op jit(solution)/shard_map/ppermute | solution.py:78
  822.6 194.7 %reduce-scatter.13.cloned.1.call-start = ((), (), s32[]{:S(2)}) async-start(), calls=%async_computation.17 | async-start | bytes 3852288
  (95 other events, 1376.0 us)
Sparse Core Ops, SparseCore 0:
  11.6 63.3 all-gather.6
  77.9 52.6 all-gather.8
  133.9 88.7 all-gather.10
  225.9 88.2 all-gather.12
  323.3 138.5 reduce-scatter.10
  467.3 148.4 reduce-scatter.8
  822.7 94.5 reduce-scatter.6
  923.0 94.2 reduce-scatter.12
